TPU v7x, 32 devices: a whole 2x2x4 slice. The times are simulated.
32 devices in a mesh: grp: 4 (over y, core), dev: 8 (over z, x).
Axes of the slice: x: 2, y: 2, z: 4, core: 2. Of those that a mesh axis runs over, the one named last changes fastest.
Arguments:
- train_grads: bfloat16 [4096, 1024], P(('grp', 'dev')), may hold values from -192 to 192, as said below
- queries: bfloat16 [512, 1024], P('grp'), may hold values from -6 to 6
Outputs:
- scores: bfloat16 [4096, 512], P(('grp', 'dev'))
Inputs may be any that keep to these rules, and one draw needn't show every extreme that they name: `train_grads`: Real-valued projected gradients whose columns and rows differ in scale.
All inputs are finite; a program needn't handle non-finite values. Where the computation divides by a largest or mean magnitude, that divisor is 1e-20 or more.
Results may differ from a plain program's by a relative error of at most 0.001.
The roundings to bfloat16 on the way count: a program that leaves them out, or rounds other values in their place, can miss the bound.
Values may be sent and summed in bfloat16 or wider, within the bound.
No kernel may reach another device: no remote copies, remote signals or barrier semaphores. Data moves between devices by JAX's collectives and lax.ppermute only.
A program may use at most 64 MiB of HBM per device.

v0:
```python
import jax
import jax.numpy as jnp
from jax import lax
from jax.sharding import PartitionSpec as P

ITERS = 8


damping_ratio = 0.1


def local_solve(gram, own, total, width):
    normed = gram / total
    damp = damping_ratio * jnp.trace(gram) / (total * width)
    bound = jnp.max(jnp.sum(jnp.abs(normed), axis=1)) + damp
    step = 1.0 / bound
    oper = normed + damp * jnp.eye(width, dtype=jnp.float32)
    state = step * own
    for index in range(ITERS):
        state = state + step * (own - jnp.dot(state, oper, precision=lax.Precision.HIGHEST))
    return state.astype(jnp.bfloat16)


def body(train_grads, queries):
    rows, width = train_grads.shape
    ndevice = lax.axis_size("dev")
    total = rows * ndevice * lax.axis_size("grp")
    qvals = queries.astype(jnp.float32)
    qrows = qvals.shape[0] // ndevice
    qstart = lax.axis_index("dev") * qrows
    own = lax.dynamic_slice_in_dim(qvals, qstart, qrows, 0)
    gram = lax.psum(
        lax.dot_general(
            train_grads, train_grads, (((0,), (0,)), ((), ())), preferred_element_type=jnp.float32
        ),
        ("grp", "dev"),
    )
    mine = local_solve(gram, own, total, width)
    prepared = lax.all_gather(mine, "dev", axis=0, tiled=True)
    return lax.dot_general(
        train_grads,
        lax.all_gather(prepared, "grp", axis=0, tiled=True),
        (((1,), (1,)), ((), ())),
        preferred_element_type=jnp.float32,
    ).astype(jnp.bfloat16)


def solution(mesh):
    return jax.shard_map(
        body,
        mesh=mesh,
        in_specs=(P(("grp", "dev"), None), P("grp", None)),
        out_specs=P(("grp", "dev"), None),
        check_vma=False,
    )
```

profile of v0, /device:TPU:0, one launch (start us, length us, event | category | flops | bytes accessed | tf_op | source)
XLA Modules:
  0.0 242.2 jit_solution(13720680544935687470)
XLA Ops:
  6.5 0.0 copy-start
  6.5 0.0 all-reduce.2.cloned.1.call-start
  6.5 0.9 copy-done
  7.5 2.7 %fusion.21 = f32[1024,1024]{1,0:T(8,128)} fusion(bf16[128,1024]{1,0:T(8,128)(2,1)S(1)} %copy-done), kind=kOutput, calls=%fused_computation.35 | convolution fusion | flops 268435456 | bytes 4456448 | tf_op jit(solution)/shard_map/dot_general | solution.py:33
  10.2 0.0 copy-start.2
  10.2 0.0 all-reduce.2.cloned.1.call-update
  10.2 0.0 all-gather.2.cloned.1.call-start
  10.3 147.6 %all-reduce.2.cloned.1.call-done = f32[1024,1024]{1,0:T(8,128)} async-done(((f32[1024,1024]{1,0:T(8,128)}), f32[1024,1024]{1,0:T(8,128)}) %all-reduce.2.cloned.1.call-update) | async-done | bytes 4194320 | tf_op jit(solution)/shard_map/psum | solution.py:32
  157.9 3.3 %select_reduce_fusion = (f32[]{:T(128)}, f32[1024]{0:T(1024)S(1)}) fusion(f32[1024,1024]{1,0:T(8,128)} %all-reduce.2.cloned.1.call-done), kind=kLoop, calls=%fused_computation.1 | loop fusion | flops 6290431 | bytes 4198404 | tf_op jit(solution)/shard_map/jit(trace)/reduce_sum | solution.py:14
  161.9 0.6 reduce_max.9
  163.2 0.0 copy-done.2
  163.2 0.0 copy-start.1
  163.2 4.6 %fusion.2 = f32[16,1024]{1,0:T(8,128)S(1)} fusion(f32[]{:T(128)S(6)} %div.15, bf16[128,1024]{1,0:T(8,128)(2,1)S(1)} %copy-done.2, s32[]{:T(128)S(6)} %select_n.9, f32[1024,1024]{1,0:T(8,128)} %all-reduce.2.cloned.1.call-done, f32[]{:T(128)S(6)} %div.14), kind=kOutput, calls=%fused_computation.15 | convolution fusion | flops 205635584 | bytes 4327936 | tf_op jit(solution)/shard_map/dot_general | solution.py:20
  167.8 0.0 copy-done.1
  167.8 2.3 fusion.4
  170.1 2.3 fusion.6
  172.3 2.3 fusion.8
  174.6 2.3 fusion.10
  176.8 2.4 %fusion.12 = f32[16,1024]{1,0:T(8,128)S(1)} fusion(f32[16,1024]{1,0:T(8,128)S(1)} %fusion.10, f32[]{:T(128)S(6)} %div.15, bf16[128,1024]{1,0:T(8,128)(2,1)S(1)} %copy-done.2, s32[]{:T(128)S(6)} %select_n.9, f32[1024,1024]{1,0:T(8,128)S(1)} %copy-done.1, f32[]{:T(128)S(6)} %div.14), kind=kOutput, calls=%fused_computation.25 | convolution fusion | flops 205586432 | bytes 4423692 | tf_op jit(solution)/shard_map/dot_general | solution.py:20
  179.3 2.3 fusion.14
  181.5 2.3 fusion.17
  183.8 32.8 %all_gather.6 = bf16[128,1024]{1,0:T(8,128)(2,1)} all-gather(bf16[16,1024]{1,0:T(8,128)(2,1)S(1)} %fusion.17), channel_id=1, replica_groups=mesh['grp'=4,'dev'=8] {'dev'}, dimensions={0}, use_global_device_ids=true | all-gather | bytes 294912 | tf_op jit(solution)/shard_map/all_gather | solution.py:39
  216.6 0.0 all-gather.2.cloned.1.call-update
  216.7 16.3 %all-gather.2.cloned.1.call-done = bf16[512,1024]{1,0:T(8,128)(2,1)} async-done(((bf16[128,1024]{1,0:T(8,128)(2,1)}), bf16[512,1024]{1,0:T(8,128)(2,1)}) %all-gather.2.cloned.1.call-update) | async-done | bytes 1048592 | tf_op jit(solution)/shard_map/all_gather | solution.py:42
  233.0 1.7 fusion
  234.6 0.8 copy.3
Async XLA Ops:
  6.5 1.0 copy-start
  6.5 151.4 %all-reduce.2.cloned.1.call-start = ((), (), s32[]{:S(2)}) async-start(), calls=%async_computation | async-start | bytes 8388608 | tf_op jit(solution)/shard_map/psum | solution.py:32
  10.2 153.0 %copy-start.2 = (bf16[128,1024]{1,0:T(8,128)(2,1)S(1)}, bf16[128,1024]{1,0:T(8,128)(2,1)}, u32[]{:S(2)}) copy-start(bf16[128,1024]{1,0:T(8,128)(2,1)} %param.3) | copy-start | bytes 786436
  10.2 222.8 %all-gather.2.cloned.1.call-start = ((), (), s32[]{:S(2)}) async-start(), calls=%async_computation.1 | async-start | bytes 1310720 | tf_op jit(solution)/shard_map/all_gather | solution.py:42
  163.2 4.6 %copy-start.1 = (f32[1024,1024]{1,0:T(8,128)S(1)}, f32[1024,1024]{1,0:T(8,128)}, u32[]{:S(2)}) copy-start(f32[1024,1024]{1,0:T(8,128)} %all-reduce.2.cloned.1.call-done) | copy-start | bytes 12582916
Sparse Core Ops, SparseCore 0:
  12.9 144.9 all-reduce.1
  216.8 16.1 all-gather.1
where the time goes:
time: 242 us
  waiting for transfers between devices  164 us (68%)
  blocking collectives  32.8 us (14%)
  matrix products  24.9 us (10%)
  between operations  14.8 us (6%)
  other arithmetic  3.94 us (2%)
    psum x1, waiting for transfers between devices, body(): lax.psum(lax.dot_general(train_grads, train_grads, (((0,), (0,)), ((), ()...  148 us
    all_gather x1, blocking collectives, body(): prepared = lax.all_gather(mine, 'dev', axis=0, tiled=True)  32.8 us
    dot_general x8, matrix products, local_solve(): jnp.dot(state, oper, precision=lax.Precision.HIGHEST)  20.5 us
    all_gather x1, waiting for transfers between devices, body(): lax.all_gather(prepared, 'grp', axis=0, tiled=True)  16.3 us
  transfers between devices with their start and end apart: 2, of which 2 were waited for; matrix products, arithmetic and copies ran while one was open for 0% of the time, Pallas kernels for 0%

commit v1 on v0

v1 whole, which is shorter than its diff:
```python
import functools
import itertools

import jax
import jax.numpy as jnp
from jax import lax
from jax.experimental import pallas as pl
from jax.experimental.pallas import tpu as pltpu
from jax.sharding import PartitionSpec as P

ITERS = 8
TILE = 128
AXES = ("grp", "dev")
GATHER_LIMIT = 8 << 20

damping_ratio = 0.1


def tri(count):
    return [(i, j) for i in range(count) for j in range(i, count)]


def load_all(refs, dest, sems):
    rows = refs[0].shape[0]
    copies = [
        pltpu.make_async_copy(ref, dest.at[pl.ds(k * rows, rows)], sems.at[k])
        for k, ref in enumerate(refs)
    ]
    for copy in copies:
        copy.start()
    for copy in copies:
        copy.wait()


def row_products(held, i):
    return lax.dot_general(
        held[:, i * TILE : (i + 1) * TILE],
        held[:, i * TILE :],
        (((0,), (0,)), ((), ())),
        preferred_element_type=jnp.float32,
    )


def gram_kernel(count, has_base, *refs):
    blocks, refs = refs[:count], refs[count:]
    base = refs[0] if has_base else None
    out, held, sems = refs[-3:]
    load_all(blocks, held, sems)
    tiles = held.shape[1] // TILE
    for i in range(tiles):
        product = row_products(held, i)
        first = i * tiles - i * (i - 1) // 2
        for j in range(i, tiles):
            part = product[:, (j - i) * TILE : (j - i + 1) * TILE]
            out[first + j - i] = part + base[first + j - i] if has_base else part


def gram_of(blocks, base=None):
    rows, width = blocks[0].shape
    shape = jax.ShapeDtypeStruct((len(tri(width // TILE)), TILE, TILE), jnp.float32)
    args = list(blocks) + ([] if base is None else [base])
    depth = rows * len(blocks)
    return pl.pallas_call(
        functools.partial(gram_kernel, len(blocks), base is not None),
        out_shape=shape,
        in_specs=[pl.BlockSpec(memory_space=pl.ANY)] * len(blocks)
        + ([] if base is None else [pl.BlockSpec(memory_space=pltpu.VMEM)]),
        out_specs=pl.BlockSpec(memory_space=pltpu.VMEM),
        scratch_shapes=[
            pltpu.VMEM((depth, width), blocks[0].dtype),
            pltpu.SemaphoreType.DMA((len(blocks),)),
        ],
        cost_estimate=pl.CostEstimate(
            flops=depth * width * width, bytes_accessed=2 * depth * width, transcendentals=0
        ),
        compiler_params=pltpu.CompilerParams(vmem_limit_bytes=40 << 20),
    )(*args)


def solve_kernel(n_sums, n_late, n_rows, total, *refs):
    sums, refs = refs[:n_sums], refs[n_sums:]
    late, refs = refs[:n_late], refs[n_late:]
    rows, refs = refs[:n_rows], refs[n_rows:]
    queries, refs = refs[0], refs[1:]
    outs, refs = refs[:n_rows], refs[n_rows:]
    high, low, spread, held, sems = refs
    width = queries.shape[1]
    tiles = width // TILE
    if n_late:
        load_all(late, held, sems)
    spread[...] = jnp.zeros_like(spread)
    diagonal = jnp.zeros((TILE, TILE), jnp.float32)
    on_diagonal = lax.broadcasted_iota(jnp.int32, (TILE, TILE), 0) == lax.broadcasted_iota(
        jnp.int32, (TILE, TILE), 1
    )

    def place(value, i, j):
        at = (slice(i * TILE, (i + 1) * TILE), slice(j * TILE, (j + 1) * TILE))
        top = value.astype(jnp.bfloat16)
        high[at] = top
        low[at] = (value - top.astype(jnp.float32)).astype(jnp.bfloat16)
        spread[at[0]] += jnp.abs(value)

    for i in range(tiles):
        product = row_products(held, i) if n_late else None
        first = i * tiles - i * (i - 1) // 2
        for j in range(i, tiles):
            value = functools.reduce(jnp.add, [s[first + j - i] for s in sums])
            if n_late:
                value = value + product[:, (j - i) * TILE : (j - i + 1) * TILE]
            place(value, i, j)
            if i == j:
                diagonal = diagonal + jnp.where(on_diagonal, value, 0.0)
            else:
                place(value.T, j, i)

    damp = damping_ratio * jnp.sum(diagonal) / (total * width)
    bound = jnp.max(jnp.sum(spread[...], axis=1, keepdims=True)) / total + damp
    step = 1.0 / bound
    scale = step / total
    keep = 1.0 - step * damp
    start = step * queries[...].astype(jnp.float32)

    def advance(_, state):
        top = state.astype(jnp.bfloat16)
        rest = (state - top.astype(jnp.float32)).astype(jnp.bfloat16)
        moved = jnp.dot(top, high[...], preferred_element_type=jnp.float32)
        moved = moved + jnp.dot(rest, high[...], preferred_element_type=jnp.float32)
        moved = moved + jnp.dot(top, low[...], preferred_element_type=jnp.float32)
        return start + (keep * state - scale * moved)

    prepared = lax.fori_loop(0, ITERS, advance, start).astype(jnp.bfloat16)
    for block, out in zip(rows, outs, strict=True):
        out[...] = lax.dot_general(
            block[...], prepared, (((1,), (1,)), ((), ())), preferred_element_type=jnp.float32
        ).astype(jnp.bfloat16)


def solve_and_score(sums, late, rows, queries, total):
    count, width = queries.shape
    depth = sum(block.shape[0] for block in late)
    return pl.pallas_call(
        functools.partial(solve_kernel, len(sums), len(late), len(rows), total),
        out_shape=[jax.ShapeDtypeStruct((block.shape[0], count), jnp.bfloat16) for block in rows],
        in_specs=[pl.BlockSpec(memory_space=pltpu.VMEM)] * len(sums)
        + [pl.BlockSpec(memory_space=pl.ANY)] * len(late)
        + [pl.BlockSpec(memory_space=pltpu.VMEM)] * (len(rows) + 1),
        out_specs=[pl.BlockSpec(memory_space=pltpu.VMEM)] * len(rows),
        scratch_shapes=[
            pltpu.VMEM((width, width), jnp.bfloat16),
            pltpu.VMEM((width, width), jnp.bfloat16),
            pltpu.VMEM((width, TILE), jnp.float32),
            pltpu.VMEM((max(depth, 16), width), jnp.bfloat16),
            pltpu.SemaphoreType.DMA((max(len(late), 1),)),
        ],
        cost_estimate=pl.CostEstimate(
            flops=6 * ITERS * count * width * width, bytes_accessed=4 * width * width, transcendentals=0
        ),
        compiler_params=pltpu.CompilerParams(vmem_limit_bytes=56 << 20),
    )(*sums, *late, *rows, queries)


def lay_kernel(count, where, *refs):
    blocks, out = refs[:count], refs[count]
    wide = blocks[0].shape[1]
    for k, block in enumerate(blocks):
        at = pl.multiple_of((where[0] ^ k) * wide, wide)
        out[:, pl.ds(at, wide)] = block[...]


def lay_out(blocks, index):
    rows, wide = blocks[0].shape
    return pl.pallas_call(
        functools.partial(lay_kernel, len(blocks)),
        out_shape=jax.ShapeDtypeStruct((rows, wide * len(blocks)), blocks[0].dtype),
        in_specs=[pl.BlockSpec(memory_space=pltpu.SMEM)]
        + [pl.BlockSpec(memory_space=pltpu.VMEM)] * len(blocks),
        out_specs=pl.BlockSpec(memory_space=pltpu.VMEM),
    )(jnp.reshape(index, (1,)).astype(jnp.int32), *blocks)


def flip(value, shape, grp_bits, dev_bits):
    n_grp, n_dev = shape
    pairs = [
        (g * n_dev + d, (g ^ grp_bits) * n_dev + (d ^ dev_bits))
        for g in range(n_grp)
        for d in range(n_dev)
    ]
    return lax.ppermute(value, AXES, pairs)


def power_of_two(value):
    return value > 0 and value & (value - 1) == 0


def routes(n_grp, n_dev):
    far = (0, n_dev // 2)
    near = [(0, 1 << k) for k in range(n_dev.bit_length() - 2)]
    near += [(1 << k, 0) for k in range(1, n_grp.bit_length() - 1)]
    near = near[:1] + near[:0:-1]
    load = {way: 2 + (way[1] == n_dev // 4) for way in near}
    found = [(far, far)] + [(way, way) for way in near]
    with_far = [((way[0] ^ far[0], way[1] ^ far[1]), way) for way in near]
    for size in range(2, len(near) + 1):
        groups = list(itertools.combinations(near, size))
        for extra in ((0, 0), far):
            for group in groups:
                offset = extra
                for way in group:
                    offset = (offset[0] ^ way[0], offset[1] ^ way[1])
                way = min(group, key=load.get)
                load[way] += 1
                found.append((offset, way))
            if size == 2 and not any(extra):
                found += with_far
    return found


def gathered_body(shape, train_grads, queries):
    n_grp, n_dev = shape
    total = train_grads.shape[0] * n_grp * n_dev
    swap = functools.partial(flip, shape=shape)

    def across(block):
        return swap(block, grp_bits=1, dev_bits=0)

    held = {(0, 0): train_grads}
    for offset, way in routes(n_grp, n_dev):
        source = held[offset[0] ^ way[0], offset[1] ^ way[1]]
        held[offset] = swap(source, grp_bits=way[0], dev_bits=way[1])
    blocks = list(held.values())
    half = (len(blocks) - 1) // 2
    first = gram_of(blocks[:half])
    mine = gram_of(blocks[half:-3], first)
    other = across(mine)
    last = blocks[-3:]
    last = last + [across(block) for block in last]
    rows = [
        across(held[k - 1, 0]) if k % 2 else held[k, 0] for k in range(n_grp)
    ]
    scores = solve_and_score([mine, other], last, rows, queries, total)
    moved = [scores[0]] + [
        swap(part, grp_bits=k, dev_bits=0) for k, part in enumerate(scores) if k
    ]
    return lay_out(moved, lax.axis_index("grp"))


def summed_body(shape, train_grads, queries):
    n_grp, n_dev = shape
    total = train_grads.shape[0] * n_grp * n_dev
    gram = lax.psum(gram_of([train_grads]), AXES)
    eye = jnp.eye(queries.shape[1], dtype=jnp.bfloat16)
    (prepared,) = solve_and_score([gram], [], [eye], queries, total)
    return lax.dot_general(
        train_grads,
        lax.all_gather(prepared, "grp", axis=1, tiled=True),
        (((1,), (0,)), ((), ())),
        preferred_element_type=jnp.float32,
    ).astype(jnp.bfloat16)


def solution(mesh):
    shape = (mesh.shape["grp"], mesh.shape["dev"])

    def body(train_grads, queries):
        rows, width = train_grads.shape
        held = rows * width * 2 * shape[0] * shape[1]
        fits = held <= GATHER_LIMIT and all(power_of_two(n) and n > 2 for n in shape)
        return (gathered_body if fits else summed_body)(shape, train_grads, queries)

    return jax.shard_map(
        body,
        mesh=mesh,
        in_specs=(P(("grp", "dev"), None), P("grp", None)),
        out_specs=P(("grp", "dev"), None),
        check_vma=False,
    )
```

time: 242 us -> 78.2 us (0.32)
  waiting for transfers between devices: 164 us -> 31.1 us
  blocking collectives: 32.8 us -> 0 us
  matrix products: 24.9 us -> 0 us
  starting transfers between devices: 0.04 us -> 22.2 us
  Pallas kernels: 0 us -> 20.9 us
  between operations: 14.8 us -> 0.16 us
  other arithmetic: 3.94 us -> 0 us
    psum x1 -> x0, waiting for transfers between devices: 148 us -> none  [body(): lax.psum(lax.dot_general(train_grads, train_grads, (((0,), (0,)), ((), ()...]
    all_gather x1 -> x0, blocking collectives: 32.8 us -> none  [body(): prepared = lax.all_gather(mine, 'dev', axis=0, tiled=True)]
    ppermute x0 -> x24, waiting for transfers between devices: none -> 31.1 us  [flip(): return lax.ppermute(value, AXES, pairs)]
    dot_general x10 -> x0, matrix products: 24.9 us -> none  [the longest x8 20.5 us: local_solve(): jnp.dot(state, oper, precision=lax.Precision.HIGHEST)]
    ppermute x0 -> x24, starting transfers between devices: none -> 22.2 us  [flip(): return lax.ppermute(value, AXES, pairs)]
    pallas_call x0 -> x4, Pallas kernels: none -> 20.9 us  [the longest x1 16.2 us: solve_and_score(): pl.pallas_call(functools.partial(solve_kernel, len(sums), len(late), len(...]
    all_gather x1 -> x0, waiting for transfers between devices: 16.3 us -> none  [body(): lax.all_gather(prepared, 'grp', axis=0, tiled=True)]
    reduce_sum x1 -> x0, other arithmetic: 3.34 us -> none  [local_solve(): damp = damping_ratio * jnp.trace(gram) / (total * width)]
  transfers between devices with their start and end apart: 2 -> 24, of which waited for: 2 -> 15; matrix products, arithmetic and copies ran while one was open for 0% -> 0% of each run, Pallas kernels for 0% -> 2%
where the time goes in v1:
time: 78.2 us; the launch traced here: 77.9 us
  waiting for transfers between devices  31.1 us (40%)
  starting transfers between devices  22.2 us (28%)
  Pallas kernels  20.9 us (27%)
  local copies, waits for them, and re-layouts  3.64 us (5%)
    ppermute x24, waiting for transfers between devices, flip(): return lax.ppermute(value, AXES, pairs)  31.1 us
    ppermute x24, starting transfers between devices, flip(): return lax.ppermute(value, AXES, pairs)  22.2 us
    pallas_call x1, Pallas kernels, solve_and_score(): pl.pallas_call(functools.partial(solve_kernel, len(sums), len(late), len(...  16.2 us
    unnamed x30, local copies, waits for them, and re-layouts  3.64 us
    pallas_call x2, Pallas kernels, gram_of(): pl.pallas_call(functools.partial(gram_kernel, len(blocks), base is not No...  3.21 us
  transfers between devices with their start and end apart: 24, of which 15 were waited for; matrix products, arithmetic and copies ran while one was open for 0% of the time, Pallas kernels for 2%

profile of v1, /device:TPU:0, one launch (start us, length us, event | category | flops | bytes accessed | tf_op | source)
XLA Modules:
  0.0 77.9 jit_solution(6264067895491950604)
XLA Ops:
  0.0 3.0 %collective-permute-start.9 = (bf16[128,1024]{1,0:T(8,128)(2,1)}, bf16[128,1024]{1,0:T(8,128)(2,1)S(1)}, u32[]{:S(2)}, u32[]{:S(2)}) collective-permute-start(bf16[128,1024]{1,0:T(8,128)(2,1)} %refs_8_.1), channel_id=1, source_target_pairs={{0,16},{1,17},{2,18},{3,19},{4,20},{5,21},{6,22},{7,23},{8,24},{9,... | collective-permute-start | bytes 786440 | tf_op jit(solution)/shard_map/ppermute | solution.py:189
  3.0 2.6 %collective-permute-start.2 = (bf16[128,1024]{1,0:T(8,128)(2,1)}, bf16[128,1024]{1,0:T(8,128)(2,1)S(1)}, u32[]{:S(2)}, u32[]{:S(2)}) collective-permute-start(bf16[128,1024]{1,0:T(8,128)(2,1)} %refs_8_.1), channel_id=1, source_target_pairs={{0,4},{1,5},{2,6},{3,7},{4,0},{5,1},{6,2},{7,3},{8,12},{9,13},{10,... | collective-permute-start | bytes 786440 | tf_op jit(solution)/shard_map/ppermute | solution.py:189
  5.6 1.6 %collective-permute-start = (bf16[128,1024]{1,0:T(8,128)(2,1)}, bf16[128,1024]{1,0:T(8,128)(2,1)S(1)}, u32[]{:S(2)}, u32[]{:S(2)}) collective-permute-start(bf16[128,1024]{1,0:T(8,128)(2,1)} %refs_8_.1), channel_id=1, source_target_pairs={{0,2},{1,3},{2,0},{3,1},{4,6},{5,7},{6,4},{7,5},{8,10},{9,11},{10,... | collective-permute-start | bytes 786440 | tf_op jit(solution)/shard_map/ppermute | solution.py:189
  7.2 1.5 %collective-permute-start.8 = (bf16[128,1024]{1,0:T(8,128)(2,1)}, bf16[128,1024]{1,0:T(8,128)(2,1)S(1)}, u32[]{:S(2)}, u32[]{:S(2)}) collective-permute-start(bf16[128,1024]{1,0:T(8,128)(2,1)} %refs_8_.1), channel_id=1, source_target_pairs={{0,1},{1,0},{2,3},{3,2},{4,5},{5,4},{6,7},{7,6},{8,9},{9,8},{10,11... | collective-permute-start | bytes 786440 | tf_op jit(solution)/shard_map/ppermute | solution.py:189
  8.7 0.9 %collective-permute-done.9.refs_3_.refs_10_ = bf16[128,1024]{1,0:T(8,128)(2,1)S(1)} collective-permute-done((bf16[128,1024]{1,0:T(8,128)(2,1)}, bf16[128,1024]{1,0:T(8,128)(2,1)S(1)}, u32[]{:S(2)}, u32[]{:S(2)}) %collective-permute-start.9) | collective-permute-done | bytes 262176 | tf_op jit(solution)/shard_map/ppermute | solution.py:189
  9.5 1.7 %collective-permute-start.10 = (bf16[128,1024]{1,0:T(8,128)(2,1)S(1)}, bf16[128,1024]{1,0:T(8,128)(2,1)S(1)}, u32[]{:S(2)}, u32[]{:S(2)}) collective-permute-start(bf16[128,1024]{1,0:T(8,128)(2,1)S(1)} %collective-permute-done.9.refs_3_.refs_10_), channel_id=1, source_target_pairs={{0,1},{1,0},{2,3},{3,2},{4,5},{5,4},{6,7},{7,6},{8,9},{9,8},{10,11... | collective-permute-start | bytes 786440 | tf_op jit(solution)/shard_map/ppermute | solution.py:189
  11.2 6.4 %collective-permute-done.2.refs_1_ = bf16[128,1024]{1,0:T(8,128)(2,1)S(1)} collective-permute-done((bf16[128,1024]{1,0:T(8,128)(2,1)}, bf16[128,1024]{1,0:T(8,128)(2,1)S(1)}, u32[]{:S(2)}, u32[]{:S(2)}) %collective-permute-start.2) | collective-permute-done | bytes 262176 | tf_op jit(solution)/shard_map/ppermute | solution.py:189
  17.6 1.5 %collective-permute-start.3 = (bf16[128,1024]{1,0:T(8,128)(2,1)S(1)}, bf16[128,1024]{1,0:T(8,128)(2,1)S(1)}, u32[]{:S(2)}, u32[]{:S(2)}) collective-permute-start(bf16[128,1024]{1,0:T(8,128)(2,1)S(1)} %collective-permute-done.2.refs_1_), channel_id=1, source_target_pairs={{0,1},{1,0},{2,3},{3,2},{4,5},{5,4},{6,7},{7,6},{8,9},{9,8},{10,11... | collective-permute-start | bytes 786440 | tf_op jit(solution)/shard_map/ppermute | solution.py:189
  19.6 1.1 %collective-permute-start.5 = (bf16[128,1024]{1,0:T(8,128)(2,1)S(1)}, bf16[128,1024]{1,0:T(8,128)(2,1)S(1)}, u32[]{:S(2)}, u32[]{:S(2)}) collective-permute-start(bf16[128,1024]{1,0:T(8,128)(2,1)S(1)} %collective-permute-done.2.refs_1_), channel_id=1, source_target_pairs={{0,2},{1,3},{2,0},{3,1},{4,6},{5,7},{6,4},{7,5},{8,10},{9,11},{10,... | collective-permute-start | bytes 786440 | tf_op jit(solution)/shard_map/ppermute | solution.py:189
  21.2 1.5 %collective-permute-start.4 = (bf16[128,1024]{1,0:T(8,128)(2,1)S(1)}, bf16[128,1024]{1,0:T(8,128)(2,1)S(1)}, u32[]{:S(2)}, u32[]{:S(2)}) collective-permute-start(bf16[128,1024]{1,0:T(8,128)(2,1)S(1)} %collective-permute-done.2.refs_1_), channel_id=1, source_target_pairs={{0,16},{1,17},{2,18},{3,19},{4,20},{5,21},{6,22},{7,23},{8,24},{9,... | collective-permute-start | bytes 786440 | tf_op jit(solution)/shard_map/ppermute | solution.py:189
  22.7 4.1 %collective-permute-done.3.refs_1_ = bf16[128,1024]{1,0:T(8,128)(2,1)S(1)} collective-permute-done((bf16[128,1024]{1,0:T(8,128)(2,1)S(1)}, bf16[128,1024]{1,0:T(8,128)(2,1)S(1)}, u32[]{:S(2)}, u32[]{:S(2)}) %collective-permute-start.3) | collective-permute-done | bytes 262176 | tf_op jit(solution)/shard_map/ppermute | solution.py:189
  27.4 4.0 %collective-permute-done.11.refs_6_ = bf16[128,1024]{1,0:T(8,128)(2,1)S(1)} collective-permute-done((bf16[128,1024]{1,0:T(8,128)(2,1)S(1)}, bf16[128,1024]{1,0:T(8,128)(2,1)S(1)}, u32[]{:S(2)}, u32[]{:S(2)}) %collective-permute-start.11) | collective-permute-done | bytes 262176 | tf_op jit(solution)/shard_map/ppermute | solution.py:189
  31.4 0.7 collective-permute-start.7
  32.1 0.9 %copy-done.1 = bf16[128,1024]{1,0:T(8,128)(2,1)S(1)} copy-done((bf16[128,1024]{1,0:T(8,128)(2,1)S(1)}, bf16[128,1024]{1,0:T(8,128)(2,1)}, u32[]{:S(2)}) %copy-start.1) | copy-done | bytes 262168
  33.1 1.8 %shard_map.28.refs_6_ = f32[36,128,128]{2,1,0:T(8,128)S(1)} custom-call(bf16[128,1024]{1,0:T(8,128)(2,1)S(1)} %copy-done.1, bf16[128,1024]{1,0:T(8,128)(2,1)S(1)} %collective-permute-done.2.refs_1_, bf16[128,1024]{1,0:T(8,128)(2,1)S(1)} %collective-permute-done.8.refs_2_, bf16[128,1024]{1,0:T(8,128)(2,1)S(1)} %collective-permute-done.9.refs_3_.refs_10_, ...), custom_call_target="tpu_custom_call" | custom-call | flops 939524096 | bytes 1835008 | tf_op jit(solution)/shard_map/pallas_call | solution.py:63
  34.9 0.6 collective-permute-done.4.refs_2_
  35.5 3.4 %collective-permute-done.6.refs_4_ = bf16[128,1024]{1,0:T(8,128)(2,1)S(1)} collective-permute-done((bf16[128,1024]{1,0:T(8,128)(2,1)S(1)}, bf16[128,1024]{1,0:T(8,128)(2,1)S(1)}, u32[]{:S(2)}, u32[]{:S(2)}) %collective-permute-start.6) | collective-permute-done | bytes 262176 | tf_op jit(solution)/shard_map/ppermute | solution.py:189
  38.9 1.4 %shard_map.29.refs_0_ = f32[36,128,128]{2,1,0:T(8,128)S(1)} custom-call(bf16[128,1024]{1,0:T(8,128)(2,1)S(1)} %collective-permute-done.1.refs_0_, bf16[128,1024]{1,0:T(8,128)(2,1)S(1)} %collective-permute-done.3.refs_1_, bf16[128,1024]{1,0:T(8,128)(2,1)S(1)} %collective-permute-done.4.refs_2_, bf16[128,1024]{1,0:T(8,128)(2,1)S(1)} %collective-permute-done.5.refs_3_, ...), custom_call_target="tpu_custom_call" | custom-call | flops 805306368 | bytes 1572864 | tf_op jit(solution)/shard_map/pallas_call | solution.py:63
  41.5 1.5 %collective-permute-start.14 = (bf16[128,1024]{1,0:T(8,128)(2,1)S(1)}, bf16[128,1024]{1,0:T(8,128)(2,1)S(1)}, u32[]{:S(2)}, u32[]{:S(2)}) collective-permute-start(bf16[128,1024]{1,0:T(8,128)(2,1)S(1)} %collective-permute-done.1.refs_0_), channel_id=1, source_target_pairs={{0,1},{1,0},{2,3},{3,2},{4,5},{5,4},{6,7},{7,6},{8,9},{9,8},{10,11... | collective-permute-start | bytes 786440 | tf_op jit(solution)/shard_map/ppermute | solution.py:189
  43.0 0.6 collective-permute-start.15
  43.5 1.8 %collective-permute-done.19.refs_9_ = bf16[128,1024]{1,0:T(8,128)(2,1)S(1)} collective-permute-done((bf16[128,1024]{1,0:T(8,128)(2,1)S(1)}, bf16[128,1024]{1,0:T(8,128)(2,1)S(1)}, u32[]{:S(2)}, u32[]{:S(2)}) %collective-permute-start.19) | collective-permute-done | bytes 262176 | tf_op jit(solution)/shard_map/ppermute | solution.py:189
  45.5 3.7 %collective-permute-done.13.refs_2_ = bf16[128,1024]{1,0:T(8,128)(2,1)S(1)} collective-permute-done((bf16[128,1024]{1,0:T(8,128)(2,1)S(1)}, bf16[128,1024]{1,0:T(8,128)(2,1)S(1)}, u32[]{:S(2)}, u32[]{:S(2)}) %collective-permute-start.13) | collective-permute-done | bytes 262176 | tf_op jit(solution)/shard_map/ppermute | solution.py:189
  49.8 0.9 %collective-permute-done.15.refs_4_ = bf16[128,1024]{1,0:T(8,128)(2,1)S(1)} collective-permute-done((bf16[128,1024]{1,0:T(8,128)(2,1)S(1)}, bf16[128,1024]{1,0:T(8,128)(2,1)S(1)}, u32[]{:S(2)}, u32[]{:S(2)}) %collective-permute-start.15) | collective-permute-done | bytes 262176 | tf_op jit(solution)/shard_map/ppermute | solution.py:189
  51.2 1.1 %collective-permute-done.18.refs_7_ = bf16[128,1024]{1,0:T(8,128)(2,1)S(1)} collective-permute-done((bf16[128,1024]{1,0:T(8,128)(2,1)S(1)}, bf16[128,1024]{1,0:T(8,128)(2,1)S(1)}, u32[]{:S(2)}, u32[]{:S(2)}) %collective-permute-start.18) | collective-permute-done | bytes 262176 | tf_op jit(solution)/shard_map/ppermute | solution.py:189
  52.3 0.6 copy-done.14
  52.9 1.4 %copy-done.6 = f32[36,128,128]{2,1,0:T(8,128)} copy-done((f32[36,128,128]{2,1,0:T(8,128)}, f32[36,128,128]{2,1,0:T(8,128)S(1)}, u32[]{:S(2)}) %copy-start.6) | copy-done | bytes 2359320
  54.4 16.2 %shard_map.30 = (bf16[128,128]{1,0:T(8,128)(2,1)}, bf16[128,128]{1,0:T(8,128)(2,1)}, bf16[128,128]{1,0:T(8,128)(2,1)}, bf16[128,128]{1,0:T(8,128)(2,1)}) custom-call(f32[36,128,128]{2,1,0:T(8,128)} %copy-done, f32[36,128,128]{2,1,0:T(8,128)} %copy-done.6, bf16[128,1024]{1,0:T(8,128)(2,1)} %copy-done.8, bf16[128,1024]{1,0:T(8,128)(2,1)} %copy-done.9, ...), custom_call_target="tpu_custom_call" | custom-call | flops 6442450944 | bytes 4194304 | tf_op jit(solution)/shard_map/pallas_call | solution.py:142
  70.7 1.5 %collective-permute-start.22 = (bf16[128,128]{1,0:T(8,128)(2,1)}, bf16[128,128]{1,0:T(8,128)(2,1)S(1)}, u32[]{:S(2)}, u32[]{:S(2)}) collective-permute-start(bf16[128,128]{1,0:T(8,128)(2,1)} %get-tuple-element.11), channel_id=1, source_target_pairs={{0,16},{1,17},{2,18},{3,19},{4,20},{5,21},{6,22},{7,23},{8,24},{9,... | collective-permute-start | bytes 98312 | tf_op jit(solution)/shard_map/ppermute | solution.py:189
  72.5 2.4 %collective-permute-done.22.refs_2_ = bf16[128,128]{1,0:T(8,128)(2,1)S(1)} collective-permute-done((bf16[128,128]{1,0:T(8,128)(2,1)}, bf16[128,128]{1,0:T(8,128)(2,1)S(1)}, u32[]{:S(2)}, u32[]{:S(2)}) %collective-permute-start.22) | collective-permute-done | bytes 32800 | tf_op jit(solution)/shard_map/ppermute | solution.py:189
  74.9 1.0 %collective-permute-done.23.refs_3_ = bf16[128,128]{1,0:T(8,128)(2,1)S(1)} collective-permute-done((bf16[128,128]{1,0:T(8,128)(2,1)}, bf16[128,128]{1,0:T(8,128)(2,1)S(1)}, u32[]{:S(2)}, u32[]{:S(2)}) %collective-permute-start.23) | collective-permute-done | bytes 32800 | tf_op jit(solution)/shard_map/ppermute | solution.py:189
  75.9 0.6 copy-done.5
  76.5 1.5 %shard_map.31 = bf16[128,512]{1,0:T(8,128)(2,1)} custom-call(s32[1]{0:T(128)} %bitcast.where, bf16[128,128]{1,0:T(8,128)(2,1)} %get-tuple-element.9.refs_0_, bf16[128,128]{1,0:T(8,128)(2,1)} %copy-done.3, bf16[128,128]{1,0:T(8,128)(2,1)} %copy-done.4, bf16[128,128]{1,0:T(8,128)(2,1)} %copy-done.5), custom_call_target="tpu_custom_call" | custom-call | tf_op jit(solution)/shard_map/pallas_call | solution.py:173
  (50 shorter events, 4.3 us)
Async XLA Ops:
  0.0 9.5 %collective-permute-start.9 = (bf16[128,1024]{1,0:T(8,128)(2,1)}, bf16[128,1024]{1,0:T(8,128)(2,1)S(1)}, u32[]{:S(2)}, u32[]{:S(2)}) collective-permute-start(bf16[128,1024]{1,0:T(8,128)(2,1)} %refs_8_.1), channel_id=1, source_target_pairs={{0,16},{1,17},{2,18},{3,19},{4,20},{5,21},{6,22},{7,23},{8,24},{9,... | collective-permute-start | bytes 786440 | tf_op jit(solution)/shard_map/ppermute | solution.py:189
  3.0 14.6 %collective-permute-start.2 = (bf16[128,1024]{1,0:T(8,128)(2,1)}, bf16[128,1024]{1,0:T(8,128)(2,1)S(1)}, u32[]{:S(2)}, u32[]{:S(2)}) collective-permute-start(bf16[128,1024]{1,0:T(8,128)(2,1)} %refs_8_.1), channel_id=1, source_target_pairs={{0,4},{1,5},{2,6},{3,7},{4,0},{5,1},{6,2},{7,3},{8,12},{9,13},{10,... | collective-permute-start | bytes 786440 | tf_op jit(solution)/shard_map/ppermute | solution.py:189
  5.6 13.5 %collective-permute-start = (bf16[128,1024]{1,0:T(8,128)(2,1)}, bf16[128,1024]{1,0:T(8,128)(2,1)S(1)}, u32[]{:S(2)}, u32[]{:S(2)}) collective-permute-start(bf16[128,1024]{1,0:T(8,128)(2,1)} %refs_8_.1), channel_id=1, source_target_pairs={{0,2},{1,3},{2,0},{3,1},{4,6},{5,7},{6,4},{7,5},{8,10},{9,11},{10,... | collective-permute-start | bytes 786440 | tf_op jit(solution)/shard_map/ppermute | solution.py:189
  7.2 13.6 %collective-permute-start.8 = (bf16[128,1024]{1,0:T(8,128)(2,1)}, bf16[128,1024]{1,0:T(8,128)(2,1)S(1)}, u32[]{:S(2)}, u32[]{:S(2)}) collective-permute-start(bf16[128,1024]{1,0:T(8,128)(2,1)} %refs_8_.1), channel_id=1, source_target_pairs={{0,1},{1,0},{2,3},{3,2},{4,5},{5,4},{6,7},{7,6},{8,9},{9,8},{10,11... | collective-permute-start | bytes 786440 | tf_op jit(solution)/shard_map/ppermute | solution.py:189
  9.5 35.8 %copy-start.2 = (bf16[128,1024]{1,0:T(8,128)(2,1)}, bf16[128,1024]{1,0:T(8,128)(2,1)S(1)}, u32[]{:S(2)}) copy-start(bf16[128,1024]{1,0:T(8,128)(2,1)S(1)} %collective-permute-done.9.refs_3_.refs_10_) | copy-start | bytes 786436
  9.5 11.7 %collective-permute-start.10 = (bf16[128,1024]{1,0:T(8,128)(2,1)S(1)}, bf16[128,1024]{1,0:T(8,128)(2,1)S(1)}, u32[]{:S(2)}, u32[]{:S(2)}) collective-permute-start(bf16[128,1024]{1,0:T(8,128)(2,1)S(1)} %collective-permute-done.9.refs_3_.refs_10_), channel_id=1, source_target_pairs={{0,1},{1,0},{2,3},{3,2},{4,5},{5,4},{6,7},{7,6},{8,9},{9,8},{10,11... | collective-permute-start | bytes 786440 | tf_op jit(solution)/shard_map/ppermute | solution.py:189
  17.6 9.2 %collective-permute-start.3 = (bf16[128,1024]{1,0:T(8,128)(2,1)S(1)}, bf16[128,1024]{1,0:T(8,128)(2,1)S(1)}, u32[]{:S(2)}, u32[]{:S(2)}) collective-permute-start(bf16[128,1024]{1,0:T(8,128)(2,1)S(1)} %collective-permute-done.2.refs_1_), channel_id=1, source_target_pairs={{0,1},{1,0},{2,3},{3,2},{4,5},{5,4},{6,7},{7,6},{8,9},{9,8},{10,11... | collective-permute-start | bytes 786440 | tf_op jit(solution)/shard_map/ppermute | solution.py:189
  19.1 12.3 %collective-permute-start.11 = (bf16[128,1024]{1,0:T(8,128)(2,1)S(1)}, bf16[128,1024]{1,0:T(8,128)(2,1)S(1)}, u32[]{:S(2)}, u32[]{:S(2)}) collective-permute-start(bf16[128,1024]{1,0:T(8,128)(2,1)S(1)} %collective-permute-done.refs_4_), channel_id=1, source_target_pairs={{0,1},{1,0},{2,3},{3,2},{4,5},{5,4},{6,7},{7,6},{8,9},{9,8},{10,11... | collective-permute-start | bytes 786440 | tf_op jit(solution)/shard_map/ppermute | solution.py:189
  19.6 15.2 %collective-permute-start.5 = (bf16[128,1024]{1,0:T(8,128)(2,1)S(1)}, bf16[128,1024]{1,0:T(8,128)(2,1)S(1)}, u32[]{:S(2)}, u32[]{:S(2)}) collective-permute-start(bf16[128,1024]{1,0:T(8,128)(2,1)S(1)} %collective-permute-done.2.refs_1_), channel_id=1, source_target_pairs={{0,2},{1,3},{2,0},{3,1},{4,6},{5,7},{6,4},{7,5},{8,10},{9,11},{10,... | collective-permute-start | bytes 786440 | tf_op jit(solution)/shard_map/ppermute | solution.py:189
  20.7 14.1 %collective-permute-start.1 = (bf16[128,1024]{1,0:T(8,128)(2,1)S(1)}, bf16[128,1024]{1,0:T(8,128)(2,1)S(1)}, u32[]{:S(2)}, u32[]{:S(2)}) collective-permute-start(bf16[128,1024]{1,0:T(8,128)(2,1)S(1)} %collective-permute-done.refs_4_), channel_id=1, source_target_pairs={{0,16},{1,17},{2,18},{3,19},{4,20},{5,21},{6,22},{7,23},{8,24},{9,... | collective-permute-start | bytes 786440 | tf_op jit(solution)/shard_map/ppermute | solution.py:189
  21.2 14.3 %collective-permute-start.4 = (bf16[128,1024]{1,0:T(8,128)(2,1)S(1)}, bf16[128,1024]{1,0:T(8,128)(2,1)S(1)}, u32[]{:S(2)}, u32[]{:S(2)}) collective-permute-start(bf16[128,1024]{1,0:T(8,128)(2,1)S(1)} %collective-permute-done.2.refs_1_), channel_id=1, source_target_pairs={{0,16},{1,17},{2,18},{3,19},{4,20},{5,21},{6,22},{7,23},{8,24},{9,... | collective-permute-start | bytes 786440 | tf_op jit(solution)/shard_map/ppermute | solution.py:189
  26.9 12.1 %collective-permute-start.6 = (bf16[128,1024]{1,0:T(8,128)(2,1)S(1)}, bf16[128,1024]{1,0:T(8,128)(2,1)S(1)}, u32[]{:S(2)}, u32[]{:S(2)}) collective-permute-start(bf16[128,1024]{1,0:T(8,128)(2,1)S(1)} %collective-permute-done.3.refs_1_), channel_id=1, source_target_pairs={{0,16},{1,17},{2,18},{3,19},{4,20},{5,21},{6,22},{7,23},{8,24},{9,... | collective-permute-start | bytes 786440 | tf_op jit(solution)/shard_map/ppermute | solution.py:189
  31.4 7.5 %collective-permute-start.7 = (bf16[128,1024]{1,0:T(8,128)(2,1)S(1)}, bf16[128,1024]{1,0:T(8,128)(2,1)S(1)}, u32[]{:S(2)}, u32[]{:S(2)}) collective-permute-start(bf16[128,1024]{1,0:T(8,128)(2,1)S(1)} %collective-permute-done.3.refs_1_), channel_id=1, source_target_pairs={{0,2},{1,3},{2,0},{3,1},{4,6},{5,7},{6,4},{7,5},{8,10},{9,11},{10,... | collective-permute-start | bytes 786440 | tf_op jit(solution)/shard_map/ppermute | solution.py:189
  40.4 11.9 %copy-start = (f32[36,128,128]{2,1,0:T(8,128)}, f32[36,128,128]{2,1,0:T(8,128)S(1)}, u32[]{:S(2)}) copy-start(f32[36,128,128]{2,1,0:T(8,128)S(1)} %shard_map.29.refs_0_) | copy-start | bytes 7077892
  40.4 11.8 %collective-permute-start.12 = (f32[36,128,128]{2,1,0:T(8,128)S(1)}, f32[36,128,128]{2,1,0:T(8,128)S(1)}, u32[]{:S(2)}, u32[]{:S(2)}) collective-permute-start(f32[36,128,128]{2,1,0:T(8,128)S(1)} %shard_map.29.refs_0_), channel_id=1, source_target_pairs={{0,8},{1,9},{2,10},{3,11},{4,12},{5,13},{6,14},{7,15},{8,0},{9,1},... | collective-permute-start | bytes 7077896 | tf_op jit(solution)/shard_map/ppermute | solution.py:189
  40.5 4.9 %collective-permute-start.19 = (bf16[128,1024]{1,0:T(8,128)(2,1)S(1)}, bf16[128,1024]{1,0:T(8,128)(2,1)S(1)}, u32[]{:S(2)}, u32[]{:S(2)}) collective-permute-start(bf16[128,1024]{1,0:T(8,128)(2,1)S(1)} %copy-done.1), channel_id=1, source_target_pairs={{0,8},{1,9},{2,10},{3,11},{4,12},{5,13},{6,14},{7,15},{8,0},{9,1},... | collective-permute-start | bytes 786440 | tf_op jit(solution)/shard_map/ppermute | solution.py:189
  41.0 8.3 %collective-permute-start.13 = (bf16[128,1024]{1,0:T(8,128)(2,1)S(1)}, bf16[128,1024]{1,0:T(8,128)(2,1)S(1)}, u32[]{:S(2)}, u32[]{:S(2)}) collective-permute-start(bf16[128,1024]{1,0:T(8,128)(2,1)S(1)} %collective-permute-done.5.refs_3_), channel_id=1, source_target_pairs={{0,16},{1,17},{2,18},{3,19},{4,20},{5,21},{6,22},{7,23},{8,24},{9,... | collective-permute-start | bytes 786440 | tf_op jit(solution)/shard_map/ppermute | solution.py:189
  41.5 8.0 %collective-permute-start.14 = (bf16[128,1024]{1,0:T(8,128)(2,1)S(1)}, bf16[128,1024]{1,0:T(8,128)(2,1)S(1)}, u32[]{:S(2)}, u32[]{:S(2)}) collective-permute-start(bf16[128,1024]{1,0:T(8,128)(2,1)S(1)} %collective-permute-done.1.refs_0_), channel_id=1, source_target_pairs={{0,1},{1,0},{2,3},{3,2},{4,5},{5,4},{6,7},{7,6},{8,9},{9,8},{10,11... | collective-permute-start | bytes 786440 | tf_op jit(solution)/shard_map/ppermute | solution.py:189
  43.0 7.7 %collective-permute-start.15 = (bf16[128,1024]{1,0:T(8,128)(2,1)S(1)}, bf16[128,1024]{1,0:T(8,128)(2,1)S(1)}, u32[]{:S(2)}, u32[]{:S(2)}) collective-permute-start(bf16[128,1024]{1,0:T(8,128)(2,1)S(1)} %collective-permute-done.6.refs_4_), channel_id=1, source_target_pairs={{0,2},{1,3},{2,0},{3,1},{4,6},{5,7},{6,4},{7,5},{8,10},{9,11},{10,... | collective-permute-start | bytes 786440 | tf_op jit(solution)/shard_map/ppermute | solution.py:189
  45.4 6.9 %copy-start.7 = (bf16[128,1024]{1,0:T(8,128)(2,1)}, bf16[128,1024]{1,0:T(8,128)(2,1)S(1)}, u32[]{:S(2)}) copy-start(bf16[128,1024]{1,0:T(8,128)(2,1)S(1)} %collective-permute-done.19.refs_9_) | copy-start | bytes 786436
  45.4 5.3 %collective-permute-start.20 = (bf16[128,1024]{1,0:T(8,128)(2,1)S(1)}, bf16[128,1024]{1,0:T(8,128)(2,1)S(1)}, u32[]{:S(2)}, u32[]{:S(2)}) collective-permute-start(bf16[128,1024]{1,0:T(8,128)(2,1)S(1)} %collective-permute-done.9.refs_3_.refs_10_), channel_id=1, source_target_pairs={{0,8},{1,9},{2,10},{3,11},{4,12},{5,13},{6,14},{7,15},{8,0},{9,1},... | collective-permute-start | bytes 786440 | tf_op jit(solution)/shard_map/ppermute | solution.py:189
  49.2 3.0 %copy-start.8 = (bf16[128,1024]{1,0:T(8,128)(2,1)}, bf16[128,1024]{1,0:T(8,128)(2,1)S(1)}, u32[]{:S(2)}) copy-start(bf16[128,1024]{1,0:T(8,128)(2,1)S(1)} %collective-permute-done.13.refs_2_) | copy-start | bytes 786436
  49.2 1.5 %collective-permute-start.16 = (bf16[128,1024]{1,0:T(8,128)(2,1)S(1)}, bf16[128,1024]{1,0:T(8,128)(2,1)S(1)}, u32[]{:S(2)}, u32[]{:S(2)}) collective-permute-start(bf16[128,1024]{1,0:T(8,128)(2,1)S(1)} %collective-permute-done.13.refs_2_), channel_id=1, source_target_pairs={{0,8},{1,9},{2,10},{3,11},{4,12},{5,13},{6,14},{7,15},{8,0},{9,1},... | collective-permute-start | bytes 786440 | tf_op jit(solution)/shard_map/ppermute | solution.py:189
  49.5 2.8 %copy-start.9 = (bf16[128,1024]{1,0:T(8,128)(2,1)}, bf16[128,1024]{1,0:T(8,128)(2,1)S(1)}, u32[]{:S(2)}) copy-start(bf16[128,1024]{1,0:T(8,128)(2,1)S(1)} %collective-permute-done.14.refs_3_) | copy-start | bytes 786436
  49.5 1.7 %collective-permute-start.17 = (bf16[128,1024]{1,0:T(8,128)(2,1)S(1)}, bf16[128,1024]{1,0:T(8,128)(2,1)S(1)}, u32[]{:S(2)}, u32[]{:S(2)}) collective-permute-start(bf16[128,1024]{1,0:T(8,128)(2,1)S(1)} %collective-permute-done.14.refs_3_), channel_id=1, source_target_pairs={{0,8},{1,9},{2,10},{3,11},{4,12},{5,13},{6,14},{7,15},{8,0},{9,1},... | collective-permute-start | bytes 786440 | tf_op jit(solution)/shard_map/ppermute | solution.py:189
  50.7 1.6 %copy-start.10 = (bf16[128,1024]{1,0:T(8,128)(2,1)}, bf16[128,1024]{1,0:T(8,128)(2,1)S(1)}, u32[]{:S(2)}) copy-start(bf16[128,1024]{1,0:T(8,128)(2,1)S(1)} %collective-permute-done.15.refs_4_) | copy-start | bytes 786436
  50.7 1.5 %collective-permute-start.18 = (bf16[128,1024]{1,0:T(8,128)(2,1)S(1)}, bf16[128,1024]{1,0:T(8,128)(2,1)S(1)}, u32[]{:S(2)}, u32[]{:S(2)}) collective-permute-start(bf16[128,1024]{1,0:T(8,128)(2,1)S(1)} %collective-permute-done.15.refs_4_), channel_id=1, source_target_pairs={{0,8},{1,9},{2,10},{3,11},{4,12},{5,13},{6,14},{7,15},{8,0},{9,1},... | collective-permute-start | bytes 786440 | tf_op jit(solution)/shard_map/ppermute | solution.py:189
  50.7 1.6 %copy-start.11 = (bf16[128,1024]{1,0:T(8,128)(2,1)}, bf16[128,1024]{1,0:T(8,128)(2,1)S(1)}, u32[]{:S(2)}) copy-start(bf16[128,1024]{1,0:T(8,128)(2,1)S(1)} %collective-permute-done.20.refs_11_) | copy-start | bytes 786436
  70.5 1.9 %collective-permute-start.21 = (bf16[128,128]{1,0:T(8,128)(2,1)}, bf16[128,128]{1,0:T(8,128)(2,1)S(1)}, u32[]{:S(2)}, u32[]{:S(2)}) collective-permute-start(bf16[128,128]{1,0:T(8,128)(2,1)} %get-tuple-element.10), channel_id=1, source_target_pairs={{0,8},{1,9},{2,10},{3,11},{4,12},{5,13},{6,14},{7,15},{8,0},{9,1},... | collective-permute-start | bytes 98312 | tf_op jit(solution)/shard_map/ppermute | solution.py:189
  70.7 4.1 %collective-permute-start.22 = (bf16[128,128]{1,0:T(8,128)(2,1)}, bf16[128,128]{1,0:T(8,128)(2,1)S(1)}, u32[]{:S(2)}, u32[]{:S(2)}) collective-permute-start(bf16[128,128]{1,0:T(8,128)(2,1)} %get-tuple-element.11), channel_id=1, source_target_pairs={{0,16},{1,17},{2,18},{3,19},{4,20},{5,21},{6,22},{7,23},{8,24},{9,... | collective-permute-start | bytes 98312 | tf_op jit(solution)/shard_map/ppermute | solution.py:189
  72.2 3.6 %collective-permute-start.23 = (bf16[128,128]{1,0:T(8,128)(2,1)}, bf16[128,128]{1,0:T(8,128)(2,1)S(1)}, u32[]{:S(2)}, u32[]{:S(2)}) collective-permute-start(bf16[128,128]{1,0:T(8,128)(2,1)} %get-tuple-element.12), channel_id=1, source_target_pairs={{0,24},{1,25},{2,26},{3,27},{4,28},{5,29},{6,30},{7,31},{8,16},{9,... | collective-permute-start | bytes 98312 | tf_op jit(solution)/shard_map/ppermute | solution.py:189
  72.5 3.4 %copy-start.3 = (bf16[128,128]{1,0:T(8,128)(2,1)}, bf16[128,128]{1,0:T(8,128)(2,1)S(1)}, u32[]{:S(2)}) copy-start(bf16[128,128]{1,0:T(8,128)(2,1)S(1)} %collective-permute-done.21.refs_1_) | copy-start | bytes 98308
  (7 other events, 7.3 us)
